TPU v7x, 256 devices: a whole 4x4x8 slice. The times are simulated.
256 devices in a mesh: inst: 8 (over x, y_lo), space: 32 (over z, y_hi, core).
Axes of the slice: x: 4, y: 4 (y_hi: 2, y_lo: 2; y = y_hi * 2 + y_lo), z: 8, core: 2. Of those that a mesh axis runs over, the one named last changes fastest.
Arguments:
- adjoint: float32 [8, 5, 256, 64, 128], P('inst', None, 'space'), may hold values from -6 to 6
- source: float32 [8, 5, 256, 64, 128], P('inst', None, 'space'), may hold values from -6 to 6
- viscosity: float32 [256, 64, 128], P('space'), may hold values from 0.2 to 2
- kappa: float32 [5], replicated, may hold values from 0.5 to 2
- coupling: float32 [5, 5], replicated, may hold values from -2.4 to 2.4
- bc_flags: int32 [5, 3], replicated, may hold values 0 or 1
- inst_map: int32 [8], replicated, may hold values from 0 to 7, each once
Outputs:
- residual: float32 [8, 5, 256, 64, 128], P('inst', None, 'space')
Inputs may be any that keep to these rules, and one draw needn't show every extreme that they name: `inst_map`: a permutation of 0 to 7. `bc_flags`: 1 marks a face of zero normal flux, 0 a face held at zero.
All inputs are finite; a program needn't handle non-finite values.
Results may differ from a plain program's by a relative error of at most 0.0001.
Values sent between devices are 32-bit elements; how exact they have to be, the bound alone decides.
A program may use at most 128 MiB of HBM per device.

v0:
```python
import jax
import jax.numpy as jnp
from jax import lax
from jax.sharding import PartitionSpec as P


def with_halo(block, sides, width):
    for axis, dim in sides:
        count = lax.axis_size(axis)
        forward = [(i, i + 1) for i in range(count - 1)]
        forward.append((count - 1, 0))
        backward = [(target, source) for source, target in forward]
        low = lax.ppermute(
            lax.slice_in_dim(block, block.shape[dim] - width, None, axis=dim), axis, forward
        )
        high = lax.ppermute(lax.slice_in_dim(block, 0, width, axis=dim), axis, backward)
        block = jnp.concatenate([low, block, high], axis=dim)
    return block


def spectral_matrix(labels, slots):
    offset = labels[:, None] - labels[None, :]
    parity = (1 - 2 * (jnp.abs(offset) % 2)).astype(jnp.float32)
    sines = jnp.sin(jnp.pi * offset.astype(jnp.float32) / slots)
    safe = jnp.where(offset == 0, jnp.float32(1.0), sines)
    return jnp.where(offset == 0, jnp.float32(0.0), 0.5 * parity / safe)


def mode_tables(points):
    indices = jnp.arange(points, dtype=jnp.int32)
    product = indices[:, None] * indices[None, :] % points
    angles = 2.0 * jnp.pi * product.astype(jnp.float32) / points
    return (jnp.cos(angles), jnp.sin(angles))


def cycle_response(points, cycle_index, near):
    indices = jnp.arange(points, dtype=jnp.int32)
    wave_number = jnp.minimum(indices, points - indices)
    cutoff = jnp.maximum(4, points * (cycle_index + 1) // (2 * near))
    return (wave_number[None, :] < cutoff[:, None]).astype(jnp.float32)


def smooth_cycles(pencil, first_cycle, near):
    points = pencil.shape[1]
    cycles = pencil.shape[2]
    cosines, sines_table = mode_tables(points)
    cycle_index = first_cycle + jnp.arange(cycles, dtype=jnp.int32)
    response = (cycle_response(points, cycle_index, near).T / points)[None, :, :, None]
    coef_cos = jnp.einsum("tk,ftrx->fkrx", cosines, pencil, precision=lax.Precision.HIGHEST)
    coef_sin = jnp.einsum("tk,ftrx->fkrx", sines_table, pencil, precision=lax.Precision.HIGHEST)
    smoothed = jnp.einsum(
        "tk,fkrx->ftrx", cosines, coef_cos * response, precision=lax.Precision.HIGHEST
    )
    smoothed = smoothed + jnp.einsum(
        "tk,fkrx->ftrx", sines_table, coef_sin * response, precision=lax.Precision.HIGHEST
    )
    weights = jnp.maximum(1.0 - cycle_index.astype(jnp.float32) / near, 0.0)[None, None, :, None]
    return pencil + weights * (smoothed - pencil)


def viscous(center, nbr_up, nbr_dn, visc, visc_up, visc_dn, kappa, flags):
    cycles = center.shape[2]
    cells_x = center.shape[3]
    cycle_weight = (1.0 / (jnp.arange(cycles, dtype=jnp.float32) + 1.0))[None, :, None]
    theta = cycle_weight * (
        0.5 * (visc + visc_up) * (center - nbr_up) + 0.5 * (visc + visc_dn) * (center - nbr_dn)
    )
    face_r = 0.5 * (visc[:, :-1, :] + visc[:, 1:, :])
    flux_r = face_r * (center[:, :, :-1, :] - center[:, :, 1:, :])
    radial = jnp.pad(flux_r, ((0, 0), (0, 0), (0, 1), (0, 0))) - jnp.pad(
        flux_r, ((0, 0), (0, 0), (1, 0), (0, 0))
    )
    face_x = 0.5 * (visc[:, :, :-1] + visc[:, :, 1:])
    flux_x = face_x * (center[:, :, :, :-1] - center[:, :, :, 1:])
    axial = jnp.pad(flux_x, ((0, 0), (0, 0), (0, 0), (0, 1))) - jnp.pad(
        flux_x, ((0, 0), (0, 0), (0, 0), (1, 0))
    )
    open_faces = (1 - flags).astype(jnp.float32)
    outer = open_faces[:, 2][:, None, None, None] * visc[None, :, -1:, :] * center[:, :, -1:, :]
    outer = jnp.pad(outer, ((0, 0), (0, 0), (cycles - 1, 0), (0, 0)))
    inflow = open_faces[:, 0][:, None, None, None] * visc[None, :, :, :1] * center[:, :, :, :1]
    inflow = jnp.pad(inflow, ((0, 0), (0, 0), (0, 0), (0, cells_x - 1)))
    outflow = open_faces[:, 1][:, None, None, None] * visc[None, :, :, -1:] * center[:, :, :, -1:]
    outflow = jnp.pad(outflow, ((0, 0), (0, 0), (0, 0), (cells_x - 1, 0)))
    return kappa[:, None, None, None] * (theta + radial + axial + outer + inflow + outflow)


def body(adjoint, source, viscosity, kappa, coupling, bc_flags, inst_map):
    slots = lax.axis_size("inst")
    own_slot = lax.axis_index("inst")
    matrix = spectral_matrix(inst_map, slots)
    center = adjoint[0]
    column = lax.dynamic_slice_in_dim(matrix, own_slot, 1, 1)[:, 0]
    spectral = jnp.tensordot(
        column,
        lax.all_gather(adjoint, "inst", axis=0, tiled=True),
        axes=1,
        precision=lax.Precision.HIGHEST,
    )
    stacked = jnp.concatenate([center, viscosity[None]], axis=0)
    padded = with_halo(stacked, (("space", 1),), 1)
    fields = center.shape[0]
    diffused = viscous(
        center,
        padded[:fields, 2:],
        padded[:fields, :-2],
        viscosity,
        padded[fields, 2:],
        padded[fields, :-2],
        kappa,
        bc_flags,
    )
    coupled = jnp.einsum("gf,gtrx->ftrx", coupling, center, precision=lax.Precision.HIGHEST)
    pre = source[0] + coupled + diffused + spectral
    total_cycles = pre.shape[2]
    near = total_cycles // 2
    pencil = lax.all_to_all(pre, "space", split_axis=2, concat_axis=1, tiled=True)
    first_cycle = lax.axis_index("space") * pencil.shape[2]
    result = smooth_cycles(pencil, first_cycle, near)
    residual = lax.all_to_all(result, "space", split_axis=1, concat_axis=2, tiled=True)
    return residual[None]


def solution(mesh):
    return jax.shard_map(
        body,
        mesh=mesh,
        in_specs=(
            P("inst", None, "space", None, None),
            P("inst", None, "space", None, None),
            P("space", None, None),
            P(),
            P(),
            P(),
            P(),
        ),
        out_specs=P("inst", None, "space", None, None),
        check_vma=False,
    )
```

profile of v0, /device:TPU:4, one launch (start us, length us, event | category | flops | bytes accessed | tf_op | source)
XLA Modules:
  0.0 363.8 jit_solution(16795134154637012902)
XLA Ops:
  6.5 0.7 all-gather.2.cloned.1.call-update
  7.3 0.6 copy-done.1
  7.9 1.6 fusion.36
  9.4 7.9 %collective-permute-start = (f32[6,1,64,128]{3,2,1,0:T(8,128)}, f32[6,1,64,128]{3,2,1,0:T(8,128)}, u32[]{:S(2)}, u32[]{:S(2)}) collective-permute-start(f32[6,1,64,128]{3,2,1,0:T(8,128)} %get-tuple-element.7), channel_id=1, source_target_pairs={{1,0},{2,1},{3,2},{4,3},{5,4},{6,5},{7,6},{8,7},{9,8},{10,9},{11,1... | collective-permute-start | bytes 589832 | tf_op jit(solution)/shard_map/ppermute | solution.py:16
  17.4 0.8 copy.120
  18.2 0.8 slice.88
  18.9 1.9 fusion.78
  20.8 1.1 copy.102
  21.9 1.1 copy.103
  23.0 1.2 pad_maximum_fusion
  24.5 1.6 fusion.14
  26.1 2.0 fusion.2
  28.1 3.7 %slice_multiply_fusion.1 = (f32[5,8,64,1]{3,0,2,1:T(8,128)}, f32[5,8,64,1]{3,0,2,1:T(8,128)}) fusion(f32[5,8,64,128]{3,0,2,1:T(8,128)S(1)} %bitcast.91, f32[8,64]{1,0:T(8,128)S(1)} %bitcast.107, f32[5]{0:T(128)S(1)} %get-tuple-element.15, f32[8,64]{1,0:T(8,128)S(1)} %bitcast.108, f32[5]{0:T(128)S(1)} %get-tuple-element.14), kind=kLoop, calls=%fused_computation.6 | loop fusion | flops 10240 | bytes 45096 | tf_op jit(solution)/shard_map/mul | solution.py:81
  31.9 1.0 copy_dynamic-update-slice_fusion.1
  33.0 0.9 copy_dynamic-update-slice_fusion
  34.2 0.9 add_multiply_fusion.2
  35.4 1.1 fusion.22
  36.5 189.8 %all-gather.2.cloned.1.call-done = f32[8,5,8,64,128]{4,3,2,1,0:T(8,128)} async-done(((f32[1,5,8,64,128]{4,3,2,1,0:T(8,128)}), f32[8,5,8,64,128]{4,3,2,1,0:T(8,128)}) %all-gather.2.cloned.1.call-update) | async-done | bytes 10485776 | tf_op jit(solution)/shard_map/all_gather | solution.py:96
  226.3 19.2 %fusion = f32[1,5,8,64,128]{4,0,3,2,1:T(1,128)S(1)} fusion(f32[8,5,8,64,128]{4,3,2,1,0:T(8,128)} %all-gather.2.cloned.1.call-done, f32[8,8]{0,1:T(8,128)S(1)} %fusion.47, s32[]{:T(128)S(6)} %select_n.41), kind=kOutput, calls=%fused_computation | convolution fusion | flops 31457280 | bytes 11796996 | tf_op jit(solution)/shard_map/dot_general | solution.py:94
  245.6 8.9 %fusion.13 = f32[5,8,64,128]{3,0,2,1:T(8,128)S(1)} fusion(f32[6,9,64,128]{3,0,2,1:T(8,128)} %copy-done.9, f32[1,5,8,64,128]{4,0,3,2,1:T(1,128)S(1)} %fusion, f32[5,8,64,128]{3,2,1,0:T(8,128)S(1)} %fusion.22, f32[1,5,8,64,128]{4,3,2,1,0:T(8,128)S(1)} %copy-done.8, f32[5,8,64,1]{3,0,2,1:T(8,128)S(1)} %copy-done.5, f32[5,8,64,1]{3,0,2,1:T(8,128)S(1)} %copy-done.4, ...), kind=kOutput, calls=%fused_computation.20 | convolution fusion | flops 24576000 | bytes 17830912 | tf_op jit(solution)/shard_map/gf,gtrx->ftrx/dot_general | solution.py:113
  254.5 1.8 copy.79
  256.4 7.6 %all-to-all-start = ((f32[5,8,64,128]{3,1,0,2:T(8,128)}), f32[5,8,64,128]{3,1,0,2:T(8,128)S(1)}, u32[]{:S(2)}, u32[]{:S(2)}) async-start(f32[5,8,64,128]{3,1,0,2:T(8,128)} %copy.79), calls=%async_computation | async-start | bytes 2621440 | tf_op jit(solution)/shard_map/all_to_all | solution.py:117
  264.1 33.9 %all-to-all-done = f32[5,8,64,128]{3,1,0,2:T(8,128)S(1)} async-done(((f32[5,8,64,128]{3,1,0,2:T(8,128)}), f32[5,8,64,128]{3,1,0,2:T(8,128)S(1)}, u32[]{:S(2)}, u32[]{:S(2)}) %all-to-all-start) | async-done | bytes 1310752 | tf_op jit(solution)/shard_map/all_to_all | solution.py:117
  298.0 1.2 copy.121
  299.1 3.2 fusion.16
  302.3 4.2 %fusion.15 = f32[5,256,2,128]{1,3,2,0:T(8,128)} fusion(f32[256,2]{0,1:T(2,128)S(1)} %compare_select_fusion, f32[5,32,8,2,128]{4,2,0,3,1:T(8,128)S(1)} %bitcast.102), kind=kOutput, calls=%fused_computation.30 | convolution fusion | flops 1007878144 | bytes 2623488 | tf_op jit(solution)/shard_map/tk,ftrx->fkrx/dot_general | solution.py:50
  306.5 1.7 copy.85
  308.2 2.2 fusion.30
  310.4 2.3 fusion.20
  312.7 1.3 copy.86
  314.0 41.2 %all_to_all.33 = f32[5,256,2,128]{3,2,0,1:T(2,128)S(1)} all-to-all(f32[5,256,2,128]{3,2,0,1:T(2,128)S(1)} %copy.86), channel_id=1, replica_groups=mesh['inst'=8,'space'=32] {'space'}, dimensions={1} | all-to-all | bytes 2621440 | tf_op jit(solution)/shard_map/all_to_all | solution.py:120
  355.4 1.3 copy.89
  (43 shorter events, 1.3 us)
Async XLA Ops:
  6.5 239.0 %copy-start = (f32[5,5]{1,0:T(8,128)S(1)}, f32[5,5]{1,0:T(8,128)}, u32[]{:S(2)}) copy-start(f32[5,5]{1,0:T(8,128)} %param.11) | copy-start | bytes 304
  6.5 1.3 copy-start.1
  6.5 219.8 %all-gather.2.cloned.1.call-start = ((), (), s32[]{:S(2)}) async-start(), calls=%async_computation.2 | async-start | bytes 11796480 | tf_op jit(solution)/shard_map/all_gather | solution.py:96
  9.4 22.5 %collective-permute-start.1 = (f32[6,1,64,128]{3,2,1,0:T(8,128)}, f32[6,1,64,128]{3,2,1,0:T(8,128)}, u32[]{:S(2)}, u32[]{:S(2)}) collective-permute-start(f32[6,1,64,128]{3,2,1,0:T(8,128)} %get-tuple-element.8), channel_id=1, source_target_pairs={{0,1},{1,2},{2,3},{3,4},{4,5},{5,6},{6,7},{7,8},{8,9},{9,10},{10,1... | collective-permute-start | bytes 589832 | tf_op jit(solution)/shard_map/ppermute | solution.py:13
  9.4 24.8 %collective-permute-start = (f32[6,1,64,128]{3,2,1,0:T(8,128)}, f32[6,1,64,128]{3,2,1,0:T(8,128)}, u32[]{:S(2)}, u32[]{:S(2)}) collective-permute-start(f32[6,1,64,128]{3,2,1,0:T(8,128)} %get-tuple-element.7), channel_id=1, source_target_pairs={{1,0},{2,1},{3,2},{4,3},{5,4},{6,5},{7,6},{8,7},{9,8},{10,9},{11,1... | collective-permute-start | bytes 589832 | tf_op jit(solution)/shard_map/ppermute | solution.py:16
  20.8 3.4 copy-start.11
  23.0 1.4 copy-start.2
  28.1 3.7 %copy-start.10 = (s32[8]{0:T(128)S(1)}, s32[8]{0:T(128)}, u32[]{:S(2)}) copy-start(s32[8]{0:T(128)} %param.13) | copy-start | bytes 100
  33.9 1.5 copy-start.9
  36.5 209.1 %copy-start.12 = (f32[5]{0:T(128)S(1)}, f32[5]{0:T(128)}, u32[]{:S(2)}) copy-start(f32[5]{0:T(128)} %param.10) | copy-start | bytes 64
  226.3 19.3 %copy-start.3 = (f32[5,8,64,127]{3,0,2,1:T(8,128)S(1)}, f32[5,8,64,127]{3,0,2,1:T(8,128)}, u32[]{:S(2)}) copy-start(f32[5,8,64,127]{3,0,2,1:T(8,128)} %fusion.2) | copy-start | bytes 3901444
  226.3 19.3 %copy-start.4 = (f32[5,8,64,1]{3,0,2,1:T(8,128)S(1)}, f32[5,8,64,1]{3,0,2,1:T(8,128)}, u32[]{:S(2)}) copy-start(f32[5,8,64,1]{3,0,2,1:T(8,128)} %get-tuple-element.5) | copy-start | bytes 30724
  226.3 19.3 %copy-start.5 = (f32[5,8,64,1]{3,0,2,1:T(8,128)S(1)}, f32[5,8,64,1]{3,0,2,1:T(8,128)}, u32[]{:S(2)}) copy-start(f32[5,8,64,1]{3,0,2,1:T(8,128)} %get-tuple-element.6) | copy-start | bytes 30724
  226.3 19.3 %copy-start.6 = (f32[5,8,63,128]{3,0,2,1:T(8,128)S(1)}, f32[5,8,63,128]{3,0,2,1:T(8,128)}, u32[]{:S(2)}) copy-start(f32[5,8,63,128]{3,0,2,1:T(8,128)} %fusion.14) | copy-start | bytes 3870724
  226.3 19.3 %copy-start.8 = (f32[1,5,8,64,128]{4,3,2,1,0:T(8,128)S(1)}, f32[1,5,8,64,128]{4,3,2,1,0:T(8,128)}, u32[]{:S(2)}) copy-start(f32[1,5,8,64,128]{4,3,2,1,0:T(8,128)} %param.8) | copy-start | bytes 3932164
  256.4 41.6 %all-to-all-start = ((f32[5,8,64,128]{3,1,0,2:T(8,128)}), f32[5,8,64,128]{3,1,0,2:T(8,128)S(1)}, u32[]{:S(2)}, u32[]{:S(2)}) async-start(f32[5,8,64,128]{3,1,0,2:T(8,128)} %copy.79), calls=%async_computation | async-start | bytes 2621440 | tf_op jit(solution)/shard_map/all_to_all | solution.py:117
  308.2 2.2 copy-start.7
Sparse Core Ops, SparseCore 0:
  9.1 217.1 all-gather.1
where the time goes:
time: 368 us; the launch traced here: 364 us
  waiting for transfers between devices  224 us (61%)
  blocking collectives  41.2 us (11%)
  matrix products  40 us (11%)
  local copies, waits for them, and re-layouts  16.2 us (4%)
  starting transfers between devices  15.5 us (4%)
  between operations  13.9 us (4%)
  other arithmetic  12.5 us (3%)
    all_gather x1, waiting for transfers between devices, body(): lax.all_gather(adjoint, 'inst', axis=0, tiled=True)  190 us
    all_to_all x1, blocking collectives, body(): lax.all_to_all(result, 'space', split_axis=1, concat_axis=2, tiled=True)  41.2 us
    all_to_all x1, waiting for transfers between devices, body(): lax.all_to_all(pre, 'space', split_axis=2, concat_axis=1, tiled=True)  33.9 us
    dot_general x1, matrix products, body(): jnp.tensordot(column, lax.all_gather(adjoint, 'inst', axis=0, tiled=True)...  19.2 us
    dot_general x1, matrix products, body(): jnp.einsum('gf,gtrx->ftrx', coupling, center, precision=lax.Precision.HIG...  8.9 us
    ppermute x1, starting transfers between devices, with_halo(): lax.ppermute(lax.slice_in_dim(block, 0, width, axis=dim), axis, backward)  7.93 us
    all_to_all x1, starting transfers between devices, body(): lax.all_to_all(pre, 'space', split_axis=2, concat_axis=1, tiled=True)  7.57 us
  transfers between devices with their start and end apart: 4, of which 2 were waited for; matrix products, arithmetic and copies ran while one was open for 6% of the time, Pallas kernels for 0%

commit v1 on v0

--- a/solution.py
+++ b/solution.py
@@ -93,7 +93,9 @@
     column = lax.dynamic_slice_in_dim(matrix, own_slot, 1, 1)[:, 0]
     spectral = jnp.tensordot(
         column,
-        lax.all_gather(adjoint, "inst", axis=0, tiled=True),
+        jnp.concatenate(
+            lax.all_to_all(jnp.stack([adjoint] * lax.axis_size("inst")), "inst", 0, 0), axis=0
+        ),
         axes=1,
         precision=lax.Precision.HIGHEST,
     )

time: 368 us -> 297 us (0.81)
  the two profiles are of different devices: /device:TPU:4 before, /device:TPU:1 now
where the time goes in v1:
time: 297 us; the launch traced here: 293 us
  waiting for transfers between devices  155 us (52%)
  blocking collectives  40.4 us (14%)
  matrix products  39.7 us (13%)
  starting transfers between devices  23.5 us (8%)
  local copies, waits for them, and re-layouts  21.9 us (7%)
  other arithmetic  11.9 us (4%)
    ppermute x1, waiting for transfers between devices, with_halo(): lax.ppermute(lax.slice_in_dim(block, block.shape[dim] - width, None, axis...  71.7 us
    all_to_all x1, waiting for transfers between devices, body(): lax.all_to_all(jnp.stack([adjoint] * lax.axis_size('inst')), 'inst', 0, 0)  48.6 us
    all_to_all x1, blocking collectives, body(): lax.all_to_all(result, 'space', split_axis=1, concat_axis=2, tiled=True)  40.4 us
    all_to_all x1, waiting for transfers between devices, body(): lax.all_to_all(pre, 'space', split_axis=2, concat_axis=1, tiled=True)  33.4 us
    dot_general x1, matrix products, body(): jnp.tensordot(column, jnp.concatenate(lax.all_to_all(jnp.stack([adjoint]...  18.9 us
    all_to_all x1, starting transfers between devices, body(): lax.all_to_all(pre, 'space', split_axis=2, concat_axis=1, tiled=True)  13.9 us
    dot_general x1, matrix products, body(): jnp.einsum('gf,gtrx->ftrx', coupling, center, precision=lax.Precision.HIG...  8.9 us
    another operation x1, local copies, waits for them, and re-layouts, body(): jnp.stack([adjoint] * lax.axis_size('inst'))  6.51 us
  transfers between devices with their start and end apart: 4, of which 4 were waited for; matrix products, arithmetic and copies ran while one was open for 7% of the time, Pallas kernels for 0%

profile of v1, /device:TPU:1, one launch (start us, length us, event | category | flops | bytes accessed | tf_op | source)
XLA Modules:
  0.0 292.6 jit_solution(18071329105246955393)
XLA Ops:
  0.0 6.5 %stack.2 = f32[8,1,5,8,64,128]{5,4,3,2,1,0:T(8,128)} broadcast(f32[5,8,64,128]{3,2,1,0:T(8,128)} %bitcast.94), dimensions={2,3,4,5} | broadcast | bytes 11796480 | tf_op jit(solution)/shard_map/stack | solution.py:97
  6.5 6.0 %all-to-all-start = ((f32[8,1,5,8,64,128]{5,4,3,2,1,0:T(8,128)}), f32[8,1,5,8,64,128]{5,4,3,2,1,0:T(8,128)}, u32[]{:S(2)}, u32[]{:S(2)}) async-start(f32[8,1,5,8,64,128]{5,4,3,2,1,0:T(8,128)} %stack.2), calls=%async_computation | async-start | bytes 20971520 | tf_op jit(solution)/shard_map/all_to_all | solution.py:97
  12.5 0.8 fusion.36
  13.3 3.6 %collective-permute-start.1 = (f32[6,1,64,128]{3,2,1,0:T(8,128)}, f32[6,1,64,128]{3,2,1,0:T(8,128)}, u32[]{:S(2)}, u32[]{:S(2)}) collective-permute-start(f32[6,1,64,128]{3,2,1,0:T(8,128)} %get-tuple-element.8), channel_id=1, source_target_pairs={{0,1},{1,2},{2,3},{3,4},{4,5},{5,6},{6,7},{7,8},{8,9},{9,10},{10,1... | collective-permute-start | bytes 589832 | tf_op jit(solution)/shard_map/ppermute | solution.py:13
  18.5 1.9 fusion.78
  20.4 1.1 copy.108
  21.5 1.1 copy.109
  22.6 1.2 pad_maximum_fusion
  24.1 1.6 fusion.14
  25.7 2.0 fusion.2
  27.7 3.9 %slice_multiply_fusion.1 = (f32[5,8,64,1]{3,0,2,1:T(8,128)}, f32[5,8,64,1]{3,0,2,1:T(8,128)}) fusion(f32[5,8,64,128]{3,0,2,1:T(8,128)S(1)} %bitcast.93, f32[8,64]{1,0:T(8,128)S(1)} %bitcast.110, f32[5]{0:T(128)S(1)} %get-tuple-element.15, f32[8,64]{1,0:T(8,128)S(1)} %bitcast.111, f32[5]{0:T(128)S(1)} %get-tuple-element.14), kind=kLoop, calls=%fused_computation.6 | loop fusion | flops 10240 | bytes 45096 | tf_op jit(solution)/shard_map/mul | solution.py:81
  31.8 71.7 %collective-permute-done.1 = f32[6,1,64,128]{3,2,1,0:T(8,128)} collective-permute-done((f32[6,1,64,128]{3,2,1,0:T(8,128)}, f32[6,1,64,128]{3,2,1,0:T(8,128)}, u32[]{:S(2)}, u32[]{:S(2)}) %collective-permute-start.1) | collective-permute-done | bytes 196640 | tf_op jit(solution)/shard_map/ppermute | solution.py:13
  103.5 1.0 copy_dynamic-update-slice_fusion.1
  104.5 0.9 copy_dynamic-update-slice_fusion
  105.7 0.9 collective-permute-done
  106.6 0.8 add_multiply_fusion.2
  107.4 1.1 fusion.22
  108.5 48.6 %all-to-all-done = f32[8,1,5,8,64,128]{5,4,3,2,1,0:T(8,128)} async-done(((f32[8,1,5,8,64,128]{5,4,3,2,1,0:T(8,128)}), f32[8,1,5,8,64,128]{5,4,3,2,1,0:T(8,128)}, u32[]{:S(2)}, u32[]{:S(2)}) %all-to-all-start) | async-done | bytes 10485792 | tf_op jit(solution)/shard_map/all_to_all | solution.py:97
  157.2 18.9 %fusion = f32[1,5,8,64,128]{4,0,3,2,1:T(1,128)S(1)} fusion(f32[8,5,8,64,128]{4,3,2,1,0:T(8,128)} %bitcast.18, f32[8,8]{0,1:T(8,128)S(1)} %fusion.47, s32[]{:T(128)S(6)} %select_n.41), kind=kOutput, calls=%fused_computation | convolution fusion | flops 31457280 | bytes 11796996 | tf_op jit(solution)/shard_map/dot_general | solution.py:94
  176.2 8.9 %fusion.13 = f32[5,8,64,128]{3,0,2,1:T(8,128)S(1)} fusion(f32[6,9,64,128]{3,0,2,1:T(8,128)} %copy-done.10, f32[1,5,8,64,128]{4,0,3,2,1:T(1,128)S(1)} %fusion, f32[5,8,64,128]{3,2,1,0:T(8,128)S(1)} %fusion.22, f32[1,5,8,64,128]{4,3,2,1,0:T(8,128)S(1)} %copy-done.9, f32[5,8,64,1]{3,0,2,1:T(8,128)S(1)} %copy-done.6, f32[5,8,64,1]{3,0,2,1:T(8,128)S(1)} %copy-done.5, ...), kind=kOutput, calls=%fused_computation.20 | convolution fusion | flops 24576000 | bytes 17830912 | tf_op jit(solution)/shard_map/gf,gtrx->ftrx/dot_general | solution.py:115
  185.1 1.8 copy.84
  186.9 13.9 %all-to-all-start.1 = ((f32[5,8,64,128]{3,1,0,2:T(8,128)}), f32[5,8,64,128]{3,1,0,2:T(8,128)S(1)}, u32[]{:S(2)}, u32[]{:S(2)}) async-start(f32[5,8,64,128]{3,1,0,2:T(8,128)} %copy.84), calls=%async_computation.1 | async-start | bytes 2621440 | tf_op jit(solution)/shard_map/all_to_all | solution.py:119
  201.0 33.4 %all-to-all-done.1 = f32[5,8,64,128]{3,1,0,2:T(8,128)S(1)} async-done(((f32[5,8,64,128]{3,1,0,2:T(8,128)}), f32[5,8,64,128]{3,1,0,2:T(8,128)S(1)}, u32[]{:S(2)}, u32[]{:S(2)}) %all-to-all-start.1) | async-done | bytes 1310752 | tf_op jit(solution)/shard_map/all_to_all | solution.py:119
  234.4 1.2 copy.127
  235.6 3.2 %fusion.16 = f32[5,256,2,128]{1,3,2,0:T(8,128)S(1)} fusion(f32[256,2]{0,1:T(2,128)S(1)} %compare_select_fusion, f32[5,32,8,2,128]{4,2,0,3,1:T(8,128)S(1)} %bitcast.104), kind=kOutput, calls=%fused_computation.32 | convolution fusion | flops 1007878144 | bytes 2623488 | tf_op jit(solution)/shard_map/tk,ftrx->fkrx/dot_general | solution.py:49
  238.7 4.2 %fusion.15 = f32[5,256,2,128]{1,3,2,0:T(8,128)} fusion(f32[256,2]{0,1:T(2,128)S(1)} %compare_select_fusion, f32[5,32,8,2,128]{4,2,0,3,1:T(8,128)S(1)} %bitcast.105), kind=kOutput, calls=%fused_computation.30 | convolution fusion | flops 1007878144 | bytes 2623488 | tf_op jit(solution)/shard_map/tk,ftrx->fkrx/dot_general | solution.py:50
  242.9 1.7 copy.90
  244.7 2.2 fusion.30
  246.9 2.3 fusion.20
  249.2 1.3 copy.91
  250.4 40.4 %all_to_all.38 = f32[5,256,2,128]{3,2,0,1:T(2,128)S(1)} all-to-all(f32[5,256,2,128]{3,2,0,1:T(2,128)S(1)} %copy.91), channel_id=1, replica_groups=mesh['inst'=8,'space'=32] {'space'}, dimensions={1} | all-to-all | bytes 2621440 | tf_op jit(solution)/shard_map/all_to_all | solution.py:122
  291.1 1.3 copy.94
  (45 shorter events, 2.6 us)
Async XLA Ops:
  0.0 176.1 %copy-start = (f32[5,5]{1,0:T(8,128)S(1)}, f32[5,5]{1,0:T(8,128)}, u32[]{:S(2)}) copy-start(f32[5,5]{1,0:T(8,128)} %param.11) | copy-start | bytes 304
  6.5 6.0 %copy-start.1 = (f32[1,5,8,64,128]{4,3,2,1,0:T(8,128)S(1)}, f32[1,5,8,64,128]{4,3,2,1,0:T(8,128)}, u32[]{:S(2)}) copy-start(f32[1,5,8,64,128]{4,3,2,1,0:T(8,128)} %param.7) | copy-start | bytes 3932164
  6.5 6.0 %copy-start.2 = (f32[8,64,128]{2,1,0:T(8,128)S(1)}, f32[8,64,128]{2,1,0:T(8,128)}, u32[]{:S(2)}) copy-start(f32[8,64,128]{2,1,0:T(8,128)} %param.9) | copy-start | bytes 786436
  6.5 150.6 %all-to-all-start = ((f32[8,1,5,8,64,128]{5,4,3,2,1,0:T(8,128)}), f32[8,1,5,8,64,128]{5,4,3,2,1,0:T(8,128)}, u32[]{:S(2)}, u32[]{:S(2)}) async-start(f32[8,1,5,8,64,128]{5,4,3,2,1,0:T(8,128)} %stack.2), calls=%async_computation | async-start | bytes 20971520 | tf_op jit(solution)/shard_map/all_to_all | solution.py:97
  13.3 90.2 %collective-permute-start.1 = (f32[6,1,64,128]{3,2,1,0:T(8,128)}, f32[6,1,64,128]{3,2,1,0:T(8,128)}, u32[]{:S(2)}, u32[]{:S(2)}) collective-permute-start(f32[6,1,64,128]{3,2,1,0:T(8,128)} %get-tuple-element.8), channel_id=1, source_target_pairs={{0,1},{1,2},{2,3},{3,4},{4,5},{5,6},{6,7},{7,8},{8,9},{9,10},{10,1... | collective-permute-start | bytes 589832 | tf_op jit(solution)/shard_map/ppermute | solution.py:13
  16.9 89.7 %collective-permute-start = (f32[6,1,64,128]{3,2,1,0:T(8,128)}, f32[6,1,64,128]{3,2,1,0:T(8,128)}, u32[]{:S(2)}, u32[]{:S(2)}) collective-permute-start(f32[6,1,64,128]{3,2,1,0:T(8,128)} %get-tuple-element.7), channel_id=1, source_target_pairs={{1,0},{2,1},{3,2},{4,3},{5,4},{6,5},{7,6},{8,7},{9,8},{10,9},{11,1... | collective-permute-start | bytes 589832 | tf_op jit(solution)/shard_map/ppermute | solution.py:16
  20.4 3.4 %copy-start.12 = (s32[5,3]{0,1:T(4,128)S(1)}, s32[5,3]{0,1:T(4,128)}, u32[]{:S(2)}) copy-start(s32[5,3]{0,1:T(4,128)} %param.12) | copy-start | bytes 184
  22.6 1.4 copy-start.3
  27.7 3.9 %copy-start.11 = (s32[8]{0:T(128)S(1)}, s32[8]{0:T(128)}, u32[]{:S(2)}) copy-start(s32[8]{0:T(128)} %param.13) | copy-start | bytes 100
  105.5 2.0 copy-start.10
  157.2 19.0 %copy-start.4 = (f32[5,8,64,127]{3,0,2,1:T(8,128)S(1)}, f32[5,8,64,127]{3,0,2,1:T(8,128)}, u32[]{:S(2)}) copy-start(f32[5,8,64,127]{3,0,2,1:T(8,128)} %fusion.2) | copy-start | bytes 3901444
  157.2 19.0 %copy-start.5 = (f32[5,8,64,1]{3,0,2,1:T(8,128)S(1)}, f32[5,8,64,1]{3,0,2,1:T(8,128)}, u32[]{:S(2)}) copy-start(f32[5,8,64,1]{3,0,2,1:T(8,128)} %get-tuple-element.5) | copy-start | bytes 30724
  157.2 19.0 %copy-start.6 = (f32[5,8,64,1]{3,0,2,1:T(8,128)S(1)}, f32[5,8,64,1]{3,0,2,1:T(8,128)}, u32[]{:S(2)}) copy-start(f32[5,8,64,1]{3,0,2,1:T(8,128)} %get-tuple-element.6) | copy-start | bytes 30724
  157.2 19.0 %copy-start.7 = (f32[5,8,63,128]{3,0,2,1:T(8,128)S(1)}, f32[5,8,63,128]{3,0,2,1:T(8,128)}, u32[]{:S(2)}) copy-start(f32[5,8,63,128]{3,0,2,1:T(8,128)} %fusion.14) | copy-start | bytes 3870724
  157.2 19.0 %copy-start.9 = (f32[1,5,8,64,128]{4,3,2,1,0:T(8,128)S(1)}, f32[1,5,8,64,128]{4,3,2,1,0:T(8,128)}, u32[]{:S(2)}) copy-start(f32[1,5,8,64,128]{4,3,2,1,0:T(8,128)} %param.8) | copy-start | bytes 3932164
  157.2 19.0 %copy-start.13 = (f32[5]{0:T(128)S(1)}, f32[5]{0:T(128)}, u32[]{:S(2)}) copy-start(f32[5]{0:T(128)} %param.10) | copy-start | bytes 64
  186.9 47.5 %all-to-all-start.1 = ((f32[5,8,64,128]{3,1,0,2:T(8,128)}), f32[5,8,64,128]{3,1,0,2:T(8,128)S(1)}, u32[]{:S(2)}, u32[]{:S(2)}) async-start(f32[5,8,64,128]{3,1,0,2:T(8,128)} %copy.84), calls=%async_computation.1 | async-start | bytes 2621440 | tf_op jit(solution)/shard_map/all_to_all | solution.py:119
  244.7 2.2 copy-start.8
